TPU v7x, 32 devices: a whole 2x2x4 slice. The times are simulated.
32 devices in a mesh: batch: 4 (over z), seq: 8 (over y, x, core).
Axes of the slice: x: 2, y: 2, z: 4, core: 2. Of those that a mesh axis runs over, the one named last changes fastest.
Arguments:
- queries: bfloat16 [16384, 8, 256], P(('batch', 'seq')), parts along dimension 0, may hold values from -400 to 400
- key_heads: bfloat16 [16384, 4, 256], P(('batch', 'seq')), parts along dimension 0, may hold values from -16 to 16
- projected_value_heads: bfloat16 [16384, 4, 256], P(('batch', 'seq')), parts along dimension 0, may hold values from -6 to 6
- lengths: int32 [4], P('batch'), parts along dimension 0, may hold values from 3585 to 4096
Outputs:
- attended: bfloat16 [16384, 8, 256], P(('batch', 'seq')), parts along dimension 0
There are 4 independent parts, one for each index of `batch`. A program takes and returns all parts, laid end to end along the dimension named above; each array names one. Nothing has to cross between parts.
All inputs are finite; a program needn't handle non-finite values.
Results may differ from a plain program's by a relative error of at most 0.0033.
Values may be sent and summed in bfloat16 or wider, within the bound.
No kernel may reach another device: no remote copies, remote signals or barrier semaphores. Data moves between devices by JAX's collectives and lax.ppermute only.
A program may use at most 192 MiB of HBM per device.

v0:
```python
import math
import jax
import jax.numpy as jnp
from jax import lax
from jax.sharding import PartitionSpec as P

WINDOW = 4096
SINKS = 4


def spread(value, axis, source):
    kept = jnp.where(lax.axis_index(axis) == source, value, 0).astype(value.dtype)
    return lax.psum(kept, axis)


def shards(queries, key_heads, projected_value_heads, lengths):
    tok_rows = queries.shape[0]
    head_count = queries.shape[1]
    head_width = queries.shape[2]
    kv_heads = key_heads.shape[1]
    share = head_count // kv_heads
    position = lax.axis_index("seq")
    length_now = lengths[0]
    first_row = position * tok_rows
    score_scale = head_width ** (-0.5)
    grouped = queries.reshape(tok_rows, kv_heads, share, head_width)
    query_pos = first_row + jnp.arange(tok_rows, dtype=jnp.int32)
    last_query = first_row + tok_rows - 1

    def attend(running, kv_block, key_start, sink_mode):
        key_count = kv_block.shape[1]
        key_pos = key_start + jnp.arange(key_count, dtype=jnp.int32)
        if sink_mode:
            useful = first_row < length_now
        else:
            useful = (
                (key_start <= last_query)
                & (key_start + key_count - 1 > first_row - WINDOW)
                & (key_start < length_now)
                & (first_row < length_now)
                & (key_start + key_count > SINKS)
            )

        def compute(current):
            maximum, totals, weighted = current
            scores = (
                jnp.einsum(
                    "qhgd,khd->hgqk", grouped, kv_block[0], preferred_element_type=jnp.float32
                )
                * score_scale
            )
            distance = query_pos[:, None] - key_pos[None, :]
            if sink_mode:
                visible = (distance >= 0) & (key_pos[None, :] < length_now)
            else:
                visible = (
                    (distance >= 0)
                    & (distance < WINDOW)
                    & (key_pos[None, :] >= SINKS)
                    & (key_pos[None, :] < length_now)
                )
            visible = visible & (query_pos[:, None] < length_now)
            masked = jnp.where(visible, scores, -1e30)
            newest = jnp.maximum(maximum, jnp.max(masked, axis=-1))
            weights = jnp.where(visible, jnp.exp(scores - newest[..., None]), 0.0)
            rescale = jnp.exp(maximum - newest)
            totals = totals * rescale + jnp.sum(weights, axis=-1)
            weighted = weighted * rescale[..., None] + jnp.einsum(
                "hgqk,khd->hgqd",
                weights.astype(jnp.bfloat16),
                kv_block[1],
                preferred_element_type=jnp.float32,
            )
            return (newest, totals, weighted)

        return lax.cond(useful, compute, lambda current: current, running)

    running = (
        jnp.full((kv_heads, share, tok_rows), -1e30, jnp.float32),
        jnp.zeros((kv_heads, share, tok_rows), jnp.float32),
        jnp.zeros((kv_heads, share, tok_rows, head_width), jnp.float32),
    )
    own_pair = jnp.stack([key_heads, projected_value_heads])
    sink_pair = spread(own_pair[:, :SINKS], "seq", 0)
    running = attend(running, sink_pair, jnp.int32(0), True)
    shard_piece = lax.all_gather(own_pair, "seq", axis=1, tiled=True)
    piece_rows = shard_piece.shape[1]
    block_size = math.gcd(piece_rows, tok_rows)

    def one_slice(slice_index, inner):
        sliced = lax.dynamic_slice_in_dim(shard_piece, slice_index * block_size, block_size, 1)
        return attend(inner, sliced, slice_index * block_size, False)

    running = lax.fori_loop(0, piece_rows // block_size, one_slice, running)
    maximum, totals, weighted = running
    valid = query_pos < length_now
    result = jnp.where(valid[:, None], weighted / jnp.where(valid, totals, 1.0)[..., None], 0.0)
    return (
        result.transpose(2, 0, 1, 3).reshape(tok_rows, head_count, head_width).astype(jnp.bfloat16)
    )


def solution(mesh):
    in_specs = (
        P(("batch", "seq"), None, None),
        P(("batch", "seq"), None, None),
        P(("batch", "seq"), None, None),
        P("batch"),
    )
    out_specs = P(("batch", "seq"), None, None)
    return jax.shard_map(shards, mesh=mesh, in_specs=in_specs, out_specs=out_specs, check_vma=False)
```

profile of v0, /device:TPU:7, one launch (start us, length us, event | category | flops | bytes accessed | tf_op | source)
XLA Modules:
  0.0 233.9 jit_solution(17987228410753566416)
XLA Ops:
  10.5 3.3 %copy.8 = bf16[512,8,256]{2,0,1:T(8,128)(2,1)} copy(bf16[512,8,256]{2,1,0:T(8,128)(2,1)} %param.10) | data formatting | bytes 4194304 | tf_op args[0]
  13.9 23.0 %psum.7 = bf16[2,4,4,256]{3,1,2,0:T(4,128)(2,1)S(1)} all-reduce(bf16[2,4,4,256]{3,1,2,0:T(4,128)(2,1)S(1)} %fusion.40), channel_id=1, replica_groups=mesh['batch'=4,'seq'=8] {'seq'}, use_global_device_ids=true, to_apply=%region_0.1 | all-reduce | flops 8192 | bytes 32768 | tf_op jit(solution)/shard_map/psum | solution.py:13
  36.9 9.0 %conditional.2 = (f32[4,2,512]{2,1,0:T(2,128)}, f32[4,2,512]{2,1,0:T(2,128)S(1)}, f32[4,2,512,256]{3,2,1,0:T(8,128)}) conditional(s32[]{:T(128)} %convert_element_type.35, () %tuple.61, (s32[512]{0:T(512)S(1)}, s32[4]{0:T(128)S(1)}, s32[]{:T(128)}, s32[4]{0:T(128)S(1)}, bf16[2,4,4,256]{3,1,2,0:T(4,128)(2,1)S(1)}, ...), branch_computations={%region_1.2_spmd, %region_2.5_spmd} | conditional | flops 17998340 | bytes 6698056 | solution.py:76
  42.8 3.2 %convolution_add_fusion = f32[4,2,512,256]{3,2,1,0:T(8,128)} fusion(f32[4,2,512]{2,1,0:T(2,128)S(1)} %get-tuple-element.538, f32[4,2,512,4]{2,3,1,0:T(4,128)S(1)} %get-tuple-element.547, f32[4,2,512]{2,1,0:T(2,128)} %get-tuple-element.637, pred[512,4]{0,1:T(4,128)(4,1)S(1)} %fusion.14, bf16[2,4,4,256]{3,1,2,0:T(4,128)(2,1)S(1)} %get-tuple-element.449), kind=kOutput, calls=%fused_computation.1 | convolution fusion | flops 9486336 | bytes 4302848 | tf_op jit(solution)/shard_map/cond/branch_1_fun/hgqk,khd->hgqd/dot_general | solution.py:68
  46.0 54.7 %all-gather.2.cloned.1.call-done = bf16[2,4096,4,256]{3,1,2,0:T(8,128)(2,1)} async-done(((bf16[2,512,4,256]{3,1,2,0:T(8,128)(2,1)}), bf16[2,4096,4,256]{3,1,2,0:T(8,128)(2,1)}) %all-gather.2.cloned.1.call-update) | async-done | bytes 16777232 | tf_op jit(solution)/shard_map/all_gather | solution.py:86
  100.6 121.3 %while.22 = (s32[]{:T(128)}, f32[4,2,512]{2,1,0:T(2,128)}, f32[4,2,512]{2,1,0:T(2,128)S(1)}, f32[4,2,512,256]{3,2,1,0:T(8,128)}, s32[]{:T(128)}, /*index=5*/s32[...) while((s32[]{:T(128)}, f32[4,2,512]{2,1,0:T(2,128)}, ...), condition=%wide.region_10.11_spmd.clone, body=%wide.region_5.10_spmd.clone.sunk | while | flops 2174495232 | bytes 39079348 | solution.py:94
  101.3 14.5 %conditional.5 = ((f32[4,2,512]{2,1,0:T(2,128)}, f32[4,2,512]{2,1,0:T(2,128)S(1)}, f32[4,2,512,256]{3,2,1,0:T(8,128)})) conditional(s32[]{:T(128)} %convert_element_type.48, (f32[4,2,512]{2,1,0:T(2,128)}, f32[4,2,512]{2,1,0:T(2,128)S(1)}, f32[4,2,512,256]{3,2,1,0:T(8,128)}) %tuple.88, (s32[]{:T(128)}, s32[]{:T(128)}, s32[512]{0:T(512)S(1)}, ...), branch_computations={%region_6.6_spmd, %region_7.9_spmd} | conditional | flops 2174495232 | bytes 39076968 | solution.py:76
  102.4 3.5 %fusion.17 = (f32[4,2,512]{2,1,0:T(2,128)S(1)}, f32[4,512,512,2]{2,1,3,0:T(8,128)S(1)}) fusion(pred[512,512]{0,1:T(8,128)(4,1)S(1)} %fusion.34, bf16[512,4,2,256]{3,0,2,1:T(8,128)(2,1)} %get-tuple-element.457, bf16[2,4096,4,256]{3,1,2,0:T(8,128)(2,1)} %get-tuple-element.456, s32[]{:T(128)S(6)} %select_n.38), kind=kOutput, calls=%fused_computation.26 | convolution fusion | flops 1080029184 | bytes 11812868 | tf_op jit(solution)/shard_map/while/body/eval_jaxpr/cond/branch_1_fun/qhgd,khd->hgqk/dot_general | solution.py:47
  109.1 6.1 %multiply_add_fusion = f32[4,2,512,256]{3,2,1,0:T(8,128)} fusion(f32[4,2,512,256]{3,2,1,0:T(8,128)} %get-tuple-element.459, f32[4,2,512]{2,1,0:T(2,128)S(1)} %bitcast.69, f32[4,512,512,2]{2,1,3,0:T(8,128)S(1)} %get-tuple-element.549, f32[4,2,512]{2,1,0:T(2,128)S(1)} %max.4, pred[512,512]{0,1:T(8,128)(4,1)S(1)} %fusion.34, ...), kind=kOutput, calls=%fused_computation.32 | convolution fusion | flops 1084227584 | bytes 18120712 | tf_op jit(solution)/shard_map/while/body/eval_jaxpr/cond/branch_1_fun/hgqk,khd->hgqd/dot_general | solution.py:68
  116.4 14.5 %conditional.5 = ((f32[4,2,512]{2,1,0:T(2,128)}, f32[4,2,512]{2,1,0:T(2,128)S(1)}, f32[4,2,512,256]{3,2,1,0:T(8,128)})) conditional(s32[]{:T(128)} %convert_element_type.48, (f32[4,2,512]{2,1,0:T(2,128)}, f32[4,2,512]{2,1,0:T(2,128)S(1)}, f32[4,2,512,256]{3,2,1,0:T(8,128)}) %tuple.88, (s32[]{:T(128)}, s32[]{:T(128)}, s32[512]{0:T(512)S(1)}, ...), branch_computations={%region_6.6_spmd, %region_7.9_spmd} | conditional | flops 2174495232 | bytes 39076968 | solution.py:76
  117.6 3.5 %fusion.17 = (f32[4,2,512]{2,1,0:T(2,128)S(1)}, f32[4,512,512,2]{2,1,3,0:T(8,128)S(1)}) fusion(pred[512,512]{0,1:T(8,128)(4,1)S(1)} %fusion.34, bf16[512,4,2,256]{3,0,2,1:T(8,128)(2,1)} %get-tuple-element.457, bf16[2,4096,4,256]{3,1,2,0:T(8,128)(2,1)} %get-tuple-element.456, s32[]{:T(128)S(6)} %select_n.38), kind=kOutput, calls=%fused_computation.26 | convolution fusion | flops 1080029184 | bytes 11812868 | tf_op jit(solution)/shard_map/while/body/eval_jaxpr/cond/branch_1_fun/qhgd,khd->hgqk/dot_general | solution.py:47
  124.2 6.1 %multiply_add_fusion = f32[4,2,512,256]{3,2,1,0:T(8,128)} fusion(f32[4,2,512,256]{3,2,1,0:T(8,128)} %get-tuple-element.459, f32[4,2,512]{2,1,0:T(2,128)S(1)} %bitcast.69, f32[4,512,512,2]{2,1,3,0:T(8,128)S(1)} %get-tuple-element.549, f32[4,2,512]{2,1,0:T(2,128)S(1)} %max.4, pred[512,512]{0,1:T(8,128)(4,1)S(1)} %fusion.34, ...), kind=kOutput, calls=%fused_computation.32 | convolution fusion | flops 1084227584 | bytes 18120712 | tf_op jit(solution)/shard_map/while/body/eval_jaxpr/cond/branch_1_fun/hgqk,khd->hgqd/dot_general | solution.py:68
  131.6 14.5 %conditional.5 = ((f32[4,2,512]{2,1,0:T(2,128)}, f32[4,2,512]{2,1,0:T(2,128)S(1)}, f32[4,2,512,256]{3,2,1,0:T(8,128)})) conditional(s32[]{:T(128)} %convert_element_type.48, (f32[4,2,512]{2,1,0:T(2,128)}, f32[4,2,512]{2,1,0:T(2,128)S(1)}, f32[4,2,512,256]{3,2,1,0:T(8,128)}) %tuple.88, (s32[]{:T(128)}, s32[]{:T(128)}, s32[512]{0:T(512)S(1)}, ...), branch_computations={%region_6.6_spmd, %region_7.9_spmd} | conditional | flops 2174495232 | bytes 39076968 | solution.py:76
  132.7 3.5 %fusion.17 = (f32[4,2,512]{2,1,0:T(2,128)S(1)}, f32[4,512,512,2]{2,1,3,0:T(8,128)S(1)}) fusion(pred[512,512]{0,1:T(8,128)(4,1)S(1)} %fusion.34, bf16[512,4,2,256]{3,0,2,1:T(8,128)(2,1)} %get-tuple-element.457, bf16[2,4096,4,256]{3,1,2,0:T(8,128)(2,1)} %get-tuple-element.456, s32[]{:T(128)S(6)} %select_n.38), kind=kOutput, calls=%fused_computation.26 | convolution fusion | flops 1080029184 | bytes 11812868 | tf_op jit(solution)/shard_map/while/body/eval_jaxpr/cond/branch_1_fun/qhgd,khd->hgqk/dot_general | solution.py:47
  139.4 6.1 %multiply_add_fusion = f32[4,2,512,256]{3,2,1,0:T(8,128)} fusion(f32[4,2,512,256]{3,2,1,0:T(8,128)} %get-tuple-element.459, f32[4,2,512]{2,1,0:T(2,128)S(1)} %bitcast.69, f32[4,512,512,2]{2,1,3,0:T(8,128)S(1)} %get-tuple-element.549, f32[4,2,512]{2,1,0:T(2,128)S(1)} %max.4, pred[512,512]{0,1:T(8,128)(4,1)S(1)} %fusion.34, ...), kind=kOutput, calls=%fused_computation.32 | convolution fusion | flops 1084227584 | bytes 18120712 | tf_op jit(solution)/shard_map/while/body/eval_jaxpr/cond/branch_1_fun/hgqk,khd->hgqd/dot_general | solution.py:68
  146.8 14.5 %conditional.5 = ((f32[4,2,512]{2,1,0:T(2,128)}, f32[4,2,512]{2,1,0:T(2,128)S(1)}, f32[4,2,512,256]{3,2,1,0:T(8,128)})) conditional(s32[]{:T(128)} %convert_element_type.48, (f32[4,2,512]{2,1,0:T(2,128)}, f32[4,2,512]{2,1,0:T(2,128)S(1)}, f32[4,2,512,256]{3,2,1,0:T(8,128)}) %tuple.88, (s32[]{:T(128)}, s32[]{:T(128)}, s32[512]{0:T(512)S(1)}, ...), branch_computations={%region_6.6_spmd, %region_7.9_spmd} | conditional | flops 2174495232 | bytes 39076968 | solution.py:76
  147.9 3.5 %fusion.17 = (f32[4,2,512]{2,1,0:T(2,128)S(1)}, f32[4,512,512,2]{2,1,3,0:T(8,128)S(1)}) fusion(pred[512,512]{0,1:T(8,128)(4,1)S(1)} %fusion.34, bf16[512,4,2,256]{3,0,2,1:T(8,128)(2,1)} %get-tuple-element.457, bf16[2,4096,4,256]{3,1,2,0:T(8,128)(2,1)} %get-tuple-element.456, s32[]{:T(128)S(6)} %select_n.38), kind=kOutput, calls=%fused_computation.26 | convolution fusion | flops 1080029184 | bytes 11812868 | tf_op jit(solution)/shard_map/while/body/eval_jaxpr/cond/branch_1_fun/qhgd,khd->hgqk/dot_general | solution.py:47
  154.6 6.1 %multiply_add_fusion = f32[4,2,512,256]{3,2,1,0:T(8,128)} fusion(f32[4,2,512,256]{3,2,1,0:T(8,128)} %get-tuple-element.459, f32[4,2,512]{2,1,0:T(2,128)S(1)} %bitcast.69, f32[4,512,512,2]{2,1,3,0:T(8,128)S(1)} %get-tuple-element.549, f32[4,2,512]{2,1,0:T(2,128)S(1)} %max.4, pred[512,512]{0,1:T(8,128)(4,1)S(1)} %fusion.34, ...), kind=kOutput, calls=%fused_computation.32 | convolution fusion | flops 1084227584 | bytes 18120712 | tf_op jit(solution)/shard_map/while/body/eval_jaxpr/cond/branch_1_fun/hgqk,khd->hgqd/dot_general | solution.py:68
  161.9 14.5 %conditional.5 = ((f32[4,2,512]{2,1,0:T(2,128)}, f32[4,2,512]{2,1,0:T(2,128)S(1)}, f32[4,2,512,256]{3,2,1,0:T(8,128)})) conditional(s32[]{:T(128)} %convert_element_type.48, (f32[4,2,512]{2,1,0:T(2,128)}, f32[4,2,512]{2,1,0:T(2,128)S(1)}, f32[4,2,512,256]{3,2,1,0:T(8,128)}) %tuple.88, (s32[]{:T(128)}, s32[]{:T(128)}, s32[512]{0:T(512)S(1)}, ...), branch_computations={%region_6.6_spmd, %region_7.9_spmd} | conditional | flops 2174495232 | bytes 39076968 | solution.py:76
  163.0 3.5 %fusion.17 = (f32[4,2,512]{2,1,0:T(2,128)S(1)}, f32[4,512,512,2]{2,1,3,0:T(8,128)S(1)}) fusion(pred[512,512]{0,1:T(8,128)(4,1)S(1)} %fusion.34, bf16[512,4,2,256]{3,0,2,1:T(8,128)(2,1)} %get-tuple-element.457, bf16[2,4096,4,256]{3,1,2,0:T(8,128)(2,1)} %get-tuple-element.456, s32[]{:T(128)S(6)} %select_n.38), kind=kOutput, calls=%fused_computation.26 | convolution fusion | flops 1080029184 | bytes 11812868 | tf_op jit(solution)/shard_map/while/body/eval_jaxpr/cond/branch_1_fun/qhgd,khd->hgqk/dot_general | solution.py:47
  169.7 6.1 %multiply_add_fusion = f32[4,2,512,256]{3,2,1,0:T(8,128)} fusion(f32[4,2,512,256]{3,2,1,0:T(8,128)} %get-tuple-element.459, f32[4,2,512]{2,1,0:T(2,128)S(1)} %bitcast.69, f32[4,512,512,2]{2,1,3,0:T(8,128)S(1)} %get-tuple-element.549, f32[4,2,512]{2,1,0:T(2,128)S(1)} %max.4, pred[512,512]{0,1:T(8,128)(4,1)S(1)} %fusion.34, ...), kind=kOutput, calls=%fused_computation.32 | convolution fusion | flops 1084227584 | bytes 18120712 | tf_op jit(solution)/shard_map/while/body/eval_jaxpr/cond/branch_1_fun/hgqk,khd->hgqd/dot_general | solution.py:68
  177.1 14.5 %conditional.5 = ((f32[4,2,512]{2,1,0:T(2,128)}, f32[4,2,512]{2,1,0:T(2,128)S(1)}, f32[4,2,512,256]{3,2,1,0:T(8,128)})) conditional(s32[]{:T(128)} %convert_element_type.48, (f32[4,2,512]{2,1,0:T(2,128)}, f32[4,2,512]{2,1,0:T(2,128)S(1)}, f32[4,2,512,256]{3,2,1,0:T(8,128)}) %tuple.88, (s32[]{:T(128)}, s32[]{:T(128)}, s32[512]{0:T(512)S(1)}, ...), branch_computations={%region_6.6_spmd, %region_7.9_spmd} | conditional | flops 2174495232 | bytes 39076968 | solution.py:76
  178.2 3.5 %fusion.17 = (f32[4,2,512]{2,1,0:T(2,128)S(1)}, f32[4,512,512,2]{2,1,3,0:T(8,128)S(1)}) fusion(pred[512,512]{0,1:T(8,128)(4,1)S(1)} %fusion.34, bf16[512,4,2,256]{3,0,2,1:T(8,128)(2,1)} %get-tuple-element.457, bf16[2,4096,4,256]{3,1,2,0:T(8,128)(2,1)} %get-tuple-element.456, s32[]{:T(128)S(6)} %select_n.38), kind=kOutput, calls=%fused_computation.26 | convolution fusion | flops 1080029184 | bytes 11812868 | tf_op jit(solution)/shard_map/while/body/eval_jaxpr/cond/branch_1_fun/qhgd,khd->hgqk/dot_general | solution.py:47
  184.9 6.1 %multiply_add_fusion = f32[4,2,512,256]{3,2,1,0:T(8,128)} fusion(f32[4,2,512,256]{3,2,1,0:T(8,128)} %get-tuple-element.459, f32[4,2,512]{2,1,0:T(2,128)S(1)} %bitcast.69, f32[4,512,512,2]{2,1,3,0:T(8,128)S(1)} %get-tuple-element.549, f32[4,2,512]{2,1,0:T(2,128)S(1)} %max.4, pred[512,512]{0,1:T(8,128)(4,1)S(1)} %fusion.34, ...), kind=kOutput, calls=%fused_computation.32 | convolution fusion | flops 1084227584 | bytes 18120712 | tf_op jit(solution)/shard_map/while/body/eval_jaxpr/cond/branch_1_fun/hgqk,khd->hgqd/dot_general | solution.py:68
  192.2 14.5 %conditional.5 = ((f32[4,2,512]{2,1,0:T(2,128)}, f32[4,2,512]{2,1,0:T(2,128)S(1)}, f32[4,2,512,256]{3,2,1,0:T(8,128)})) conditional(s32[]{:T(128)} %convert_element_type.48, (f32[4,2,512]{2,1,0:T(2,128)}, f32[4,2,512]{2,1,0:T(2,128)S(1)}, f32[4,2,512,256]{3,2,1,0:T(8,128)}) %tuple.88, (s32[]{:T(128)}, s32[]{:T(128)}, s32[512]{0:T(512)S(1)}, ...), branch_computations={%region_6.6_spmd, %region_7.9_spmd} | conditional | flops 2174495232 | bytes 39076968 | solution.py:76
  193.4 3.5 %fusion.17 = (f32[4,2,512]{2,1,0:T(2,128)S(1)}, f32[4,512,512,2]{2,1,3,0:T(8,128)S(1)}) fusion(pred[512,512]{0,1:T(8,128)(4,1)S(1)} %fusion.34, bf16[512,4,2,256]{3,0,2,1:T(8,128)(2,1)} %get-tuple-element.457, bf16[2,4096,4,256]{3,1,2,0:T(8,128)(2,1)} %get-tuple-element.456, s32[]{:T(128)S(6)} %select_n.38), kind=kOutput, calls=%fused_computation.26 | convolution fusion | flops 1080029184 | bytes 11812868 | tf_op jit(solution)/shard_map/while/body/eval_jaxpr/cond/branch_1_fun/qhgd,khd->hgqk/dot_general | solution.py:47
  200.0 6.1 %multiply_add_fusion = f32[4,2,512,256]{3,2,1,0:T(8,128)} fusion(f32[4,2,512,256]{3,2,1,0:T(8,128)} %get-tuple-element.459, f32[4,2,512]{2,1,0:T(2,128)S(1)} %bitcast.69, f32[4,512,512,2]{2,1,3,0:T(8,128)S(1)} %get-tuple-element.549, f32[4,2,512]{2,1,0:T(2,128)S(1)} %max.4, pred[512,512]{0,1:T(8,128)(4,1)S(1)} %fusion.34, ...), kind=kOutput, calls=%fused_computation.32 | convolution fusion | flops 1084227584 | bytes 18120712 | tf_op jit(solution)/shard_map/while/body/eval_jaxpr/cond/branch_1_fun/hgqk,khd->hgqd/dot_general | solution.py:68
  207.4 14.5 %conditional.5 = ((f32[4,2,512]{2,1,0:T(2,128)}, f32[4,2,512]{2,1,0:T(2,128)S(1)}, f32[4,2,512,256]{3,2,1,0:T(8,128)})) conditional(s32[]{:T(128)} %convert_element_type.48, (f32[4,2,512]{2,1,0:T(2,128)}, f32[4,2,512]{2,1,0:T(2,128)S(1)}, f32[4,2,512,256]{3,2,1,0:T(8,128)}) %tuple.88, (s32[]{:T(128)}, s32[]{:T(128)}, s32[512]{0:T(512)S(1)}, ...), branch_computations={%region_6.6_spmd, %region_7.9_spmd} | conditional | flops 2174495232 | bytes 39076968 | solution.py:76
  208.5 3.5 %fusion.17 = (f32[4,2,512]{2,1,0:T(2,128)S(1)}, f32[4,512,512,2]{2,1,3,0:T(8,128)S(1)}) fusion(pred[512,512]{0,1:T(8,128)(4,1)S(1)} %fusion.34, bf16[512,4,2,256]{3,0,2,1:T(8,128)(2,1)} %get-tuple-element.457, bf16[2,4096,4,256]{3,1,2,0:T(8,128)(2,1)} %get-tuple-element.456, s32[]{:T(128)S(6)} %select_n.38), kind=kOutput, calls=%fused_computation.26 | convolution fusion | flops 1080029184 | bytes 11812868 | tf_op jit(solution)/shard_map/while/body/eval_jaxpr/cond/branch_1_fun/qhgd,khd->hgqk/dot_general | solution.py:47
  215.2 6.1 %multiply_add_fusion = f32[4,2,512,256]{3,2,1,0:T(8,128)} fusion(f32[4,2,512,256]{3,2,1,0:T(8,128)} %get-tuple-element.459, f32[4,2,512]{2,1,0:T(2,128)S(1)} %bitcast.69, f32[4,512,512,2]{2,1,3,0:T(8,128)S(1)} %get-tuple-element.549, f32[4,2,512]{2,1,0:T(2,128)S(1)} %max.4, pred[512,512]{0,1:T(8,128)(4,1)S(1)} %fusion.34, ...), kind=kOutput, calls=%fused_computation.32 | convolution fusion | flops 1084227584 | bytes 18120712 | tf_op jit(solution)/shard_map/while/body/eval_jaxpr/cond/branch_1_fun/hgqk,khd->hgqd/dot_general | solution.py:68
  221.9 2.6 %select_convert_fusion = bf16[4,2,512,256]{3,2,1,0:T(8,128)(2,1)S(1)} fusion(f32[4,2,512,256]{3,2,1,0:T(8,128)} %get-tuple-element.483, f32[4,2,512]{2,1,0:T(2,128)S(1)} %broadcast_select_fusion, pred[512]{0:T(512)(128)(4,1)S(1)} %broadcast_compare_fusion.5), kind=kLoop, calls=%fused_computation.57 | loop fusion | flops 3145728 | bytes 6308352 | tf_op jit(solution)/shard_map/convert_element_type | solution.py:99
  224.5 2.5 %copy.15 = bf16[512,8,256]{2,1,0:T(8,128)(2,1)} copy(bf16[512,8,256]{2,0,1:T(8,128)(2,1)S(1)} %bitcast.66) | data formatting | bytes 4194304 | tf_op jit(solution)/shard_map/convert_element_type | solution.py:99
  (80 shorter events, 48.2 us)
Async XLA Ops:
  6.5 94.1 %all-gather.2.cloned.1.call-start = ((), (), s32[]{:S(2)}) async-start(), calls=%async_computation | async-start | bytes 18874368 | tf_op jit(solution)/shard_map/all_gather | solution.py:86
Sparse Core Ops, SparseCore 0:
  10.0 90.5 all-gather.1
where the time goes:
time: 236 us; the launch traced here: 234 us
  matrix products  81.8 us (35%)
  waiting for transfers between devices  54.7 us (23%)
  other arithmetic  41.9 us (18%)
  blocking collectives  23 us (10%)
  between operations  14.1 us (6%)
  local copies, waits for them, and re-layouts  12.5 us (5%)
  loops' own time  5.89 us (2%)
    all_gather x1, waiting for transfers between devices, shards(): shard_piece = lax.all_gather(own_pair, 'seq', axis=1, tiled=True)  54.7 us
    dot_general x9, matrix products, compute(): jnp.einsum('hgqk,khd->hgqd', weights.astype(jnp.bfloat16), kv_block[1], p...  51.9 us
    dot_general x9, matrix products, compute(): jnp.einsum('qhgd,khd->hgqk', grouped, kv_block[0], preferred_element_type...  29.9 us
    psum x1, blocking collectives, spread(): return lax.psum(kept, axis)  23 us
    reduce_sum x9, other arithmetic, compute(): totals = totals * rescale + jnp.sum(weights, axis=-1)  14.7 us
    add x9, other arithmetic, compute(): totals = totals * rescale + jnp.sum(weights, axis=-1)  6.6 us
    lt x9, other arithmetic, compute(): visible = visible & (query_pos[:, None] < length_now)  5.88 us
    max x8, other arithmetic, compute(): newest = jnp.maximum(maximum, jnp.max(masked, axis=-1))  5.86 us
  transfers between devices with their start and end apart: 1, of which 1 were waited for; matrix products, arithmetic and copies ran while one was open for 5% of the time, Pallas kernels for 0%

commit v1 on v0

--- a/solution.py
+++ b/solution.py
@@ -83,7 +83,12 @@
     own_pair = jnp.stack([key_heads, projected_value_heads])
     sink_pair = spread(own_pair[:, :SINKS], "seq", 0)
     running = attend(running, sink_pair, jnp.int32(0), True)
-    shard_piece = lax.all_gather(own_pair, "seq", axis=1, tiled=True)
+    ring = [own_pair]
+    for hop in range(7):
+        ring.append(lax.ppermute(ring[-1], "seq", [(dev, (dev + 1) % 8) for dev in range(8)]))
+    shard_piece = jnp.roll(
+        jnp.concatenate(ring[::-1], axis=1), (lax.axis_index("seq") + 1) * ring[0].shape[1], axis=1
+    )
     piece_rows = shard_piece.shape[1]
     block_size = math.gcd(piece_rows, tok_rows)
 

time: 236 us -> 410 us (1.74)
  waiting for transfers between devices: 54.7 us -> 138 us
  local copies, waits for them, and re-layouts: 12.5 us -> 60.5 us
  matrix products: 81.8 us -> 103 us
  starting transfers between devices: 0.01 us -> 20.4 us
  blocking collectives: 23 us -> 36.6 us
  between operations: 14.1 us -> 0.93 us
    ppermute x0 -> x7, waiting for transfers between devices: none -> 138 us  [shards(): lax.ppermute(ring[-1], 'seq', [(dev, (dev + 1) % 8) for dev in range(8)])]
    all_gather x1 -> x0, waiting for transfers between devices: 54.7 us -> none  [shards(): shard_piece = lax.all_gather(own_pair, 'seq', axis=1, tiled=True)]
    dot_general x9, matrix products: 51.9 us -> 78.7 us  [compute(): jnp.einsum('hgqk,khd->hgqd', weights.astype(jnp.bfloat16), kv_block[1], p...]
    unnamed x1 -> x33, local copies, waits for them, and re-layouts: 3.34 us -> 25.2 us
    ppermute x0 -> x7, starting transfers between devices: none -> 20.4 us  [shards(): lax.ppermute(ring[-1], 'seq', [(dev, (dev + 1) % 8) for dev in range(8)])]
    cond x8 -> x24, local copies, waits for them, and re-layouts: 4.78 us -> 24.4 us
    psum x1, blocking collectives: 23 us -> 36.6 us  [spread(): return lax.psum(kept, axis)]
    dynamic_slice x0 -> x1, local copies, waits for them, and re-layouts: none -> 6.54 us  [shards(): jnp.roll(jnp.concatenate(ring[::-1], axis=1), (lax.axis_index('seq') + 1)...]
  transfers between devices with their start and end apart: 1 -> 7, of which waited for: 1 -> 6; matrix products, arithmetic and copies ran while one was open for 5% -> 3% of each run, Pallas kernels for 0% -> 0%
where the time goes in v1:
time: 410 us; the launch traced here: 407 us
  waiting for transfers between devices  138 us (34%)
  matrix products  103 us (25%)
  local copies, waits for them, and re-layouts  60.5 us (15%)
  other arithmetic  41.3 us (10%)
  blocking collectives  36.6 us (9%)
  starting transfers between devices  20.4 us (5%)
  loops' own time  6.17 us (2%)
    ppermute x7, waiting for transfers between devices, shards(): lax.ppermute(ring[-1], 'seq', [(dev, (dev + 1) % 8) for dev in range(8)])  138 us
    dot_general x9, matrix products, compute(): jnp.einsum('hgqk,khd->hgqd', weights.astype(jnp.bfloat16), kv_block[1], p...  78.7 us
    psum x1, blocking collectives, spread(): return lax.psum(kept, axis)  36.6 us
    unnamed x33, local copies, waits for them, and re-layouts  25.2 us
    cond x24, local copies, waits for them, and re-layouts  24.4 us
    dot_general x9, matrix products, compute(): jnp.einsum('qhgd,khd->hgqk', grouped, kv_block[0], preferred_element_type...  24.3 us
    ppermute x7, starting transfers between devices, shards(): lax.ppermute(ring[-1], 'seq', [(dev, (dev + 1) % 8) for dev in range(8)])  20.4 us
    reduce_sum x9, other arithmetic, compute(): totals = totals * rescale + jnp.sum(weights, axis=-1)  14.9 us
  transfers between devices with their start and end apart: 7, of which 6 were waited for; matrix products, arithmetic and copies ran while one was open for 3% of the time, Pallas kernels for 0%

profile of v1, /device:TPU:7, one launch (start us, length us, event | category | flops | bytes accessed | tf_op | source)
XLA Modules:
  0.0 406.7 jit_solution(1135281862366831605)
XLA Ops:
  2.1 23.0 %collective-permute-done = bf16[2,512,4,256]{3,1,2,0:T(8,128)(2,1)S(1)} collective-permute-done((bf16[2,512,4,256]{3,1,2,0:T(8,128)(2,1)S(1)}, bf16[2,512,4,256]{3,1,2,0:T(8,128)(2,1)S(1)}, u32[]{:S(2)}, u32[]{:S(2)}) %collective-permute-start) | collective-permute-done | bytes 2097184 | tf_op jit(solution)/shard_map/ppermute | solution.py:88
  26.4 3.4 collective-permute-start.1
  29.8 23.0 %collective-permute-done.1 = bf16[2,512,4,256]{3,1,2,0:T(8,128)(2,1)S(1)} collective-permute-done((bf16[2,512,4,256]{3,1,2,0:T(8,128)(2,1)S(1)}, bf16[2,512,4,256]{3,1,2,0:T(8,128)(2,1)S(1)}, u32[]{:S(2)}, u32[]{:S(2)}) %collective-permute-start.1) | collective-permute-done | bytes 2097184 | tf_op jit(solution)/shard_map/ppermute | solution.py:88
  54.1 3.4 collective-permute-start.2
  57.5 23.0 %collective-permute-done.2 = bf16[2,512,4,256]{3,1,2,0:T(8,128)(2,1)S(1)} collective-permute-done((bf16[2,512,4,256]{3,1,2,0:T(8,128)(2,1)S(1)}, bf16[2,512,4,256]{3,1,2,0:T(8,128)(2,1)S(1)}, u32[]{:S(2)}, u32[]{:S(2)}) %collective-permute-start.2) | collective-permute-done | bytes 2097184 | tf_op jit(solution)/shard_map/ppermute | solution.py:88
  81.8 3.4 collective-permute-start.3
  85.1 23.0 %collective-permute-done.3 = bf16[2,512,4,256]{3,1,2,0:T(8,128)(2,1)S(1)} collective-permute-done((bf16[2,512,4,256]{3,1,2,0:T(8,128)(2,1)S(1)}, bf16[2,512,4,256]{3,1,2,0:T(8,128)(2,1)S(1)}, u32[]{:S(2)}, u32[]{:S(2)}) %collective-permute-start.3) | collective-permute-done | bytes 2097184 | tf_op jit(solution)/shard_map/ppermute | solution.py:88
  109.5 3.4 collective-permute-start.4
  112.8 23.0 %collective-permute-done.4 = bf16[2,512,4,256]{3,1,2,0:T(8,128)(2,1)S(1)} collective-permute-done((bf16[2,512,4,256]{3,1,2,0:T(8,128)(2,1)S(1)}, bf16[2,512,4,256]{3,1,2,0:T(8,128)(2,1)S(1)}, u32[]{:S(2)}, u32[]{:S(2)}) %collective-permute-start.4) | collective-permute-done | bytes 2097184 | tf_op jit(solution)/shard_map/ppermute | solution.py:88
  137.2 3.4 collective-permute-start.5
  140.5 23.0 %collective-permute-done.5 = bf16[2,512,4,256]{3,1,2,0:T(8,128)(2,1)} collective-permute-done((bf16[2,512,4,256]{3,1,2,0:T(8,128)(2,1)S(1)}, bf16[2,512,4,256]{3,1,2,0:T(8,128)(2,1)}, u32[]{:S(2)}, u32[]{:S(2)}) %collective-permute-start.5) | collective-permute-done | bytes 2097184 | tf_op jit(solution)/shard_map/ppermute | solution.py:88
  163.5 3.5 collective-permute-start.6
  171.0 36.6 %psum.7 = bf16[2,4,4,256]{3,1,2,0:T(4,128)(2,1)S(1)} all-reduce(bf16[2,4,4,256]{3,1,2,0:T(4,128)(2,1)S(1)} %fusion.40), channel_id=1, replica_groups=mesh['batch'=4,'seq'=8] {'seq'}, use_global_device_ids=true, to_apply=%region_0.1 | all-reduce | flops 8192 | bytes 32768 | tf_op jit(solution)/shard_map/psum | solution.py:13
  207.6 9.2 %conditional.2 = (f32[4,2,512]{2,1,0:T(2,128)}, f32[4,2,512]{2,1,0:T(2,128)S(1)}, f32[4,2,512,256]{3,2,1,0:T(8,128)}) conditional(s32[]{:T(128)} %convert_element_type.35, () %tuple.61, (s32[512]{0:T(512)S(1)}, s32[4]{0:T(128)S(1)}, s32[]{:T(128)}, s32[4]{0:T(128)S(1)}, bf16[2,4,4,256]{3,1,2,0:T(4,128)(2,1)S(1)}, ...), branch_computations={%region_1.2_spmd, %region_2.5_spmd} | conditional | flops 17998340 | bytes 6698056 | solution.py:76
  232.6 6.5 %constant_dynamic-slice_fusion = bf16[2,4096,4,256]{3,1,2,0:T(8,128)(2,1)} fusion(bf16[2,8192,4,256]{3,1,2,0:T(8,128)(2,1)S(1)} %constant_dynamic-update-slice_fusion, s32[]{:T(128)S(6)} %select_n.61), kind=kLoop, calls=%fused_computation.84 | loop fusion | bytes 33554436 | tf_op jit(solution)/shard_map/jit(_roll_dynamic)/dynamic_slice | solution.py:89
  239.1 162.5 %while.22 = (s32[]{:T(128)}, f32[4,2,512]{2,1,0:T(2,128)}, f32[4,2,512]{2,1,0:T(2,128)S(1)}, f32[4,2,512,256]{3,2,1,0:T(8,128)}, s32[]{:T(128)}, /*index=5*/s32[...) while((s32[]{:T(128)}, f32[4,2,512]{2,1,0:T(2,128)}, ...), condition=%wide.region_10.11_spmd.clone, body=%wide.region_5.10_spmd.clone.sunk | while | flops 2174495232 | bytes 72633808 | solution.py:99
  239.8 19.6 %conditional.5 = ((f32[4,2,512]{2,1,0:T(2,128)}, f32[4,2,512]{2,1,0:T(2,128)S(1)}, f32[4,2,512,256]{3,2,1,0:T(8,128)})) conditional(s32[]{:T(128)} %convert_element_type.48, (f32[4,2,512]{2,1,0:T(2,128)}, f32[4,2,512]{2,1,0:T(2,128)S(1)}, f32[4,2,512,256]{3,2,1,0:T(8,128)}) %tuple.88, (s32[]{:T(128)}, s32[]{:T(128)}, s32[512]{0:T(512)S(1)}, ...), branch_computations={%region_6.6_spmd, %region_7.9_spmd} | conditional | flops 2174495232 | bytes 72631424 | solution.py:76
  249.4 9.4 %multiply_add_fusion = f32[4,2,512,256]{3,2,1,0:T(8,128)} fusion(f32[4,2,512,256]{3,2,1,0:T(8,128)} %get-tuple-element.459, f32[4,2,512]{2,1,0:T(2,128)S(1)} %bitcast.69, f32[4,512,512,2]{2,1,3,0:T(8,128)} %copy-done, f32[4,2,512]{2,1,0:T(2,128)S(1)} %max.4, pred[512,512]{0,1:T(8,128)(4,1)S(1)} %fusion.34, ...), kind=kOutput, calls=%fused_computation.32 | convolution fusion | flops 1084227584 | bytes 18120712 | tf_op jit(solution)/shard_map/while/body/eval_jaxpr/cond/branch_1_fun/hgqk,khd->hgqd/dot_general | solution.py:68
  260.1 19.6 %conditional.5 = ((f32[4,2,512]{2,1,0:T(2,128)}, f32[4,2,512]{2,1,0:T(2,128)S(1)}, f32[4,2,512,256]{3,2,1,0:T(8,128)})) conditional(s32[]{:T(128)} %convert_element_type.48, (f32[4,2,512]{2,1,0:T(2,128)}, f32[4,2,512]{2,1,0:T(2,128)S(1)}, f32[4,2,512,256]{3,2,1,0:T(8,128)}) %tuple.88, (s32[]{:T(128)}, s32[]{:T(128)}, s32[512]{0:T(512)S(1)}, ...), branch_computations={%region_6.6_spmd, %region_7.9_spmd} | conditional | flops 2174495232 | bytes 72631424 | solution.py:76
  269.7 9.4 %multiply_add_fusion = f32[4,2,512,256]{3,2,1,0:T(8,128)} fusion(f32[4,2,512,256]{3,2,1,0:T(8,128)} %get-tuple-element.459, f32[4,2,512]{2,1,0:T(2,128)S(1)} %bitcast.69, f32[4,512,512,2]{2,1,3,0:T(8,128)} %copy-done, f32[4,2,512]{2,1,0:T(2,128)S(1)} %max.4, pred[512,512]{0,1:T(8,128)(4,1)S(1)} %fusion.34, ...), kind=kOutput, calls=%fused_computation.32 | convolution fusion | flops 1084227584 | bytes 18120712 | tf_op jit(solution)/shard_map/while/body/eval_jaxpr/cond/branch_1_fun/hgqk,khd->hgqd/dot_general | solution.py:68
  280.4 19.6 %conditional.5 = ((f32[4,2,512]{2,1,0:T(2,128)}, f32[4,2,512]{2,1,0:T(2,128)S(1)}, f32[4,2,512,256]{3,2,1,0:T(8,128)})) conditional(s32[]{:T(128)} %convert_element_type.48, (f32[4,2,512]{2,1,0:T(2,128)}, f32[4,2,512]{2,1,0:T(2,128)S(1)}, f32[4,2,512,256]{3,2,1,0:T(8,128)}) %tuple.88, (s32[]{:T(128)}, s32[]{:T(128)}, s32[512]{0:T(512)S(1)}, ...), branch_computations={%region_6.6_spmd, %region_7.9_spmd} | conditional | flops 2174495232 | bytes 72631424 | solution.py:76
  290.0 9.4 %multiply_add_fusion = f32[4,2,512,256]{3,2,1,0:T(8,128)} fusion(f32[4,2,512,256]{3,2,1,0:T(8,128)} %get-tuple-element.459, f32[4,2,512]{2,1,0:T(2,128)S(1)} %bitcast.69, f32[4,512,512,2]{2,1,3,0:T(8,128)} %copy-done, f32[4,2,512]{2,1,0:T(2,128)S(1)} %max.4, pred[512,512]{0,1:T(8,128)(4,1)S(1)} %fusion.34, ...), kind=kOutput, calls=%fused_computation.32 | convolution fusion | flops 1084227584 | bytes 18120712 | tf_op jit(solution)/shard_map/while/body/eval_jaxpr/cond/branch_1_fun/hgqk,khd->hgqd/dot_general | solution.py:68
  300.7 19.6 %conditional.5 = ((f32[4,2,512]{2,1,0:T(2,128)}, f32[4,2,512]{2,1,0:T(2,128)S(1)}, f32[4,2,512,256]{3,2,1,0:T(8,128)})) conditional(s32[]{:T(128)} %convert_element_type.48, (f32[4,2,512]{2,1,0:T(2,128)}, f32[4,2,512]{2,1,0:T(2,128)S(1)}, f32[4,2,512,256]{3,2,1,0:T(8,128)}) %tuple.88, (s32[]{:T(128)}, s32[]{:T(128)}, s32[512]{0:T(512)S(1)}, ...), branch_computations={%region_6.6_spmd, %region_7.9_spmd} | conditional | flops 2174495232 | bytes 72631424 | solution.py:76
  310.3 9.4 %multiply_add_fusion = f32[4,2,512,256]{3,2,1,0:T(8,128)} fusion(f32[4,2,512,256]{3,2,1,0:T(8,128)} %get-tuple-element.459, f32[4,2,512]{2,1,0:T(2,128)S(1)} %bitcast.69, f32[4,512,512,2]{2,1,3,0:T(8,128)} %copy-done, f32[4,2,512]{2,1,0:T(2,128)S(1)} %max.4, pred[512,512]{0,1:T(8,128)(4,1)S(1)} %fusion.34, ...), kind=kOutput, calls=%fused_computation.32 | convolution fusion | flops 1084227584 | bytes 18120712 | tf_op jit(solution)/shard_map/while/body/eval_jaxpr/cond/branch_1_fun/hgqk,khd->hgqd/dot_general | solution.py:68
  321.0 19.6 %conditional.5 = ((f32[4,2,512]{2,1,0:T(2,128)}, f32[4,2,512]{2,1,0:T(2,128)S(1)}, f32[4,2,512,256]{3,2,1,0:T(8,128)})) conditional(s32[]{:T(128)} %convert_element_type.48, (f32[4,2,512]{2,1,0:T(2,128)}, f32[4,2,512]{2,1,0:T(2,128)S(1)}, f32[4,2,512,256]{3,2,1,0:T(8,128)}) %tuple.88, (s32[]{:T(128)}, s32[]{:T(128)}, s32[512]{0:T(512)S(1)}, ...), branch_computations={%region_6.6_spmd, %region_7.9_spmd} | conditional | flops 2174495232 | bytes 72631424 | solution.py:76
  330.6 9.4 %multiply_add_fusion = f32[4,2,512,256]{3,2,1,0:T(8,128)} fusion(f32[4,2,512,256]{3,2,1,0:T(8,128)} %get-tuple-element.459, f32[4,2,512]{2,1,0:T(2,128)S(1)} %bitcast.69, f32[4,512,512,2]{2,1,3,0:T(8,128)} %copy-done, f32[4,2,512]{2,1,0:T(2,128)S(1)} %max.4, pred[512,512]{0,1:T(8,128)(4,1)S(1)} %fusion.34, ...), kind=kOutput, calls=%fused_computation.32 | convolution fusion | flops 1084227584 | bytes 18120712 | tf_op jit(solution)/shard_map/while/body/eval_jaxpr/cond/branch_1_fun/hgqk,khd->hgqd/dot_general | solution.py:68
  341.3 19.6 %conditional.5 = ((f32[4,2,512]{2,1,0:T(2,128)}, f32[4,2,512]{2,1,0:T(2,128)S(1)}, f32[4,2,512,256]{3,2,1,0:T(8,128)})) conditional(s32[]{:T(128)} %convert_element_type.48, (f32[4,2,512]{2,1,0:T(2,128)}, f32[4,2,512]{2,1,0:T(2,128)S(1)}, f32[4,2,512,256]{3,2,1,0:T(8,128)}) %tuple.88, (s32[]{:T(128)}, s32[]{:T(128)}, s32[512]{0:T(512)S(1)}, ...), branch_computations={%region_6.6_spmd, %region_7.9_spmd} | conditional | flops 2174495232 | bytes 72631424 | solution.py:76
  350.9 9.4 %multiply_add_fusion = f32[4,2,512,256]{3,2,1,0:T(8,128)} fusion(f32[4,2,512,256]{3,2,1,0:T(8,128)} %get-tuple-element.459, f32[4,2,512]{2,1,0:T(2,128)S(1)} %bitcast.69, f32[4,512,512,2]{2,1,3,0:T(8,128)} %copy-done, f32[4,2,512]{2,1,0:T(2,128)S(1)} %max.4, pred[512,512]{0,1:T(8,128)(4,1)S(1)} %fusion.34, ...), kind=kOutput, calls=%fused_computation.32 | convolution fusion | flops 1084227584 | bytes 18120712 | tf_op jit(solution)/shard_map/while/body/eval_jaxpr/cond/branch_1_fun/hgqk,khd->hgqd/dot_general | solution.py:68
  361.6 19.6 %conditional.5 = ((f32[4,2,512]{2,1,0:T(2,128)}, f32[4,2,512]{2,1,0:T(2,128)S(1)}, f32[4,2,512,256]{3,2,1,0:T(8,128)})) conditional(s32[]{:T(128)} %convert_element_type.48, (f32[4,2,512]{2,1,0:T(2,128)}, f32[4,2,512]{2,1,0:T(2,128)S(1)}, f32[4,2,512,256]{3,2,1,0:T(8,128)}) %tuple.88, (s32[]{:T(128)}, s32[]{:T(128)}, s32[512]{0:T(512)S(1)}, ...), branch_computations={%region_6.6_spmd, %region_7.9_spmd} | conditional | flops 2174495232 | bytes 72631424 | solution.py:76
  371.2 9.4 %multiply_add_fusion = f32[4,2,512,256]{3,2,1,0:T(8,128)} fusion(f32[4,2,512,256]{3,2,1,0:T(8,128)} %get-tuple-element.459, f32[4,2,512]{2,1,0:T(2,128)S(1)} %bitcast.69, f32[4,512,512,2]{2,1,3,0:T(8,128)} %copy-done, f32[4,2,512]{2,1,0:T(2,128)S(1)} %max.4, pred[512,512]{0,1:T(8,128)(4,1)S(1)} %fusion.34, ...), kind=kOutput, calls=%fused_computation.32 | convolution fusion | flops 1084227584 | bytes 18120712 | tf_op jit(solution)/shard_map/while/body/eval_jaxpr/cond/branch_1_fun/hgqk,khd->hgqd/dot_general | solution.py:68
  381.9 19.6 %conditional.5 = ((f32[4,2,512]{2,1,0:T(2,128)}, f32[4,2,512]{2,1,0:T(2,128)S(1)}, f32[4,2,512,256]{3,2,1,0:T(8,128)})) conditional(s32[]{:T(128)} %convert_element_type.48, (f32[4,2,512]{2,1,0:T(2,128)}, f32[4,2,512]{2,1,0:T(2,128)S(1)}, f32[4,2,512,256]{3,2,1,0:T(8,128)}) %tuple.88, (s32[]{:T(128)}, s32[]{:T(128)}, s32[512]{0:T(512)S(1)}, ...), branch_computations={%region_6.6_spmd, %region_7.9_spmd} | conditional | flops 2174495232 | bytes 72631424 | solution.py:76
  391.5 9.4 %multiply_add_fusion = f32[4,2,512,256]{3,2,1,0:T(8,128)} fusion(f32[4,2,512,256]{3,2,1,0:T(8,128)} %get-tuple-element.459, f32[4,2,512]{2,1,0:T(2,128)S(1)} %bitcast.69, f32[4,512,512,2]{2,1,3,0:T(8,128)} %copy-done, f32[4,2,512]{2,1,0:T(2,128)S(1)} %max.4, pred[512,512]{0,1:T(8,128)(4,1)S(1)} %fusion.34, ...), kind=kOutput, calls=%fused_computation.32 | convolution fusion | flops 1084227584 | bytes 18120712 | tf_op jit(solution)/shard_map/while/body/eval_jaxpr/cond/branch_1_fun/hgqk,khd->hgqd/dot_general | solution.py:68
  (142 shorter events, 122.8 us)
Async XLA Ops:
  2.0 23.0 %collective-permute-start = (bf16[2,512,4,256]{3,1,2,0:T(8,128)(2,1)S(1)}, bf16[2,512,4,256]{3,1,2,0:T(8,128)(2,1)S(1)}, u32[]{:S(2)}, u32[]{:S(2)}) collective-permute-start(bf16[2,512,4,256]{3,1,2,0:T(8,128)(2,1)S(1)} %pad_maximum_fusion), channel_id=1, source_target_pairs={{0,1},{1,2},{2,3},{3,4},{4,5},{5,6},{6,7},{7,0},{8,9},{9,10},{10,1... | collective-permute-start | bytes 6291464 | tf_op jit(solution)/shard_map/ppermute | solution.py:88
  25.1 1.3 copy-start.2
  26.4 26.4 %collective-permute-start.1 = (bf16[2,512,4,256]{3,1,2,0:T(8,128)(2,1)S(1)}, bf16[2,512,4,256]{3,1,2,0:T(8,128)(2,1)S(1)}, u32[]{:S(2)}, u32[]{:S(2)}) collective-permute-start(bf16[2,512,4,256]{3,1,2,0:T(8,128)(2,1)S(1)} %collective-permute-done), channel_id=1, source_target_pairs={{0,1},{1,2},{2,3},{3,4},{4,5},{5,6},{6,7},{7,0},{8,9},{9,10},{10,1... | collective-permute-start | bytes 6291464 | tf_op jit(solution)/shard_map/ppermute | solution.py:88
  52.7 1.3 copy-start.4
  54.1 26.4 %collective-permute-start.2 = (bf16[2,512,4,256]{3,1,2,0:T(8,128)(2,1)S(1)}, bf16[2,512,4,256]{3,1,2,0:T(8,128)(2,1)S(1)}, u32[]{:S(2)}, u32[]{:S(2)}) collective-permute-start(bf16[2,512,4,256]{3,1,2,0:T(8,128)(2,1)S(1)} %collective-permute-done.1), channel_id=1, source_target_pairs={{0,1},{1,2},{2,3},{3,4},{4,5},{5,6},{6,7},{7,0},{8,9},{9,10},{10,1... | collective-permute-start | bytes 6291464 | tf_op jit(solution)/shard_map/ppermute | solution.py:88
  80.4 1.3 copy-start.6
  81.8 26.4 %collective-permute-start.3 = (bf16[2,512,4,256]{3,1,2,0:T(8,128)(2,1)S(1)}, bf16[2,512,4,256]{3,1,2,0:T(8,128)(2,1)S(1)}, u32[]{:S(2)}, u32[]{:S(2)}) collective-permute-start(bf16[2,512,4,256]{3,1,2,0:T(8,128)(2,1)S(1)} %collective-permute-done.2), channel_id=1, source_target_pairs={{0,1},{1,2},{2,3},{3,4},{4,5},{5,6},{6,7},{7,0},{8,9},{9,10},{10,1... | collective-permute-start | bytes 6291464 | tf_op jit(solution)/shard_map/ppermute | solution.py:88
  108.1 1.3 copy-start.8
  109.5 26.4 %collective-permute-start.4 = (bf16[2,512,4,256]{3,1,2,0:T(8,128)(2,1)S(1)}, bf16[2,512,4,256]{3,1,2,0:T(8,128)(2,1)S(1)}, u32[]{:S(2)}, u32[]{:S(2)}) collective-permute-start(bf16[2,512,4,256]{3,1,2,0:T(8,128)(2,1)S(1)} %collective-permute-done.3), channel_id=1, source_target_pairs={{0,1},{1,2},{2,3},{3,4},{4,5},{5,6},{6,7},{7,0},{8,9},{9,10},{10,1... | collective-permute-start | bytes 6291464 | tf_op jit(solution)/shard_map/ppermute | solution.py:88
  135.8 1.3 copy-start.9
  137.2 26.4 %collective-permute-start.5 = (bf16[2,512,4,256]{3,1,2,0:T(8,128)(2,1)S(1)}, bf16[2,512,4,256]{3,1,2,0:T(8,128)(2,1)}, u32[]{:S(2)}, u32[]{:S(2)}) collective-permute-start(bf16[2,512,4,256]{3,1,2,0:T(8,128)(2,1)S(1)} %collective-permute-done.4), channel_id=1, source_target_pairs={{0,1},{1,2},{2,3},{3,4},{4,5},{5,6},{6,7},{7,0},{8,9},{9,10},{10,1... | collective-permute-start | bytes 6291464 | tf_op jit(solution)/shard_map/ppermute | solution.py:88
  163.5 53.3 %collective-permute-start.6 = (bf16[2,512,4,256]{3,1,2,0:T(8,128)(2,1)}, bf16[2,512,4,256]{3,1,2,0:T(8,128)(2,1)}, u32[]{:S(2)}, u32[]{:S(2)}) collective-permute-start(bf16[2,512,4,256]{3,1,2,0:T(8,128)(2,1)} %collective-permute-done.5), channel_id=1, source_target_pairs={{0,1},{1,2},{2,3},{3,4},{4,5},{5,6},{6,7},{7,0},{8,9},{9,10},{10,1... | collective-permute-start | bytes 6291464 | tf_op jit(solution)/shard_map/ppermute | solution.py:88
  216.9 7.5 %copy-start.7 = (bf16[2,512,4,256]{3,1,2,0:T(8,128)(2,1)S(1)}, bf16[2,512,4,256]{3,1,2,0:T(8,128)(2,1)}, u32[]{:S(2)}) copy-start(bf16[2,512,4,256]{3,1,2,0:T(8,128)(2,1)} %copy-done.6) | copy-start | bytes 6291460
  218.8 5.7 %copy-start.5 = (bf16[2,512,4,256]{3,1,2,0:T(8,128)(2,1)S(1)}, bf16[2,512,4,256]{3,1,2,0:T(8,128)(2,1)}, u32[]{:S(2)}) copy-start(bf16[2,512,4,256]{3,1,2,0:T(8,128)(2,1)} %copy-done.4) | copy-start | bytes 6291460
  220.7 4.0 copy-start.3
  232.5 6.6 %copy-start.1 = (bf16[512,8,256]{2,0,1:T(8,128)(2,1)S(1)}, bf16[512,8,256]{2,0,1:T(8,128)(2,1)}, u32[]{:S(2)}) copy-start(bf16[512,8,256]{2,0,1:T(8,128)(2,1)} %copy.8) | copy-start | bytes 6291460
  243.7 3.2 copy-start
  264.0 3.2 copy-start
  284.3 3.2 copy-start
  304.6 3.2 copy-start
  324.9 3.2 copy-start
  345.2 3.2 copy-start
  365.5 3.2 copy-start
  385.8 3.2 copy-start
